TPU v7x, 32 devices: a whole 2x2x4 slice. The times are simulated.
32 devices in a mesh: grp: 2 (over y), band: 4 (over z), strm: 4 (over x, core).
Axes of the slice: x: 2, y: 2, z: 4, core: 2. Of those that a mesh axis runs over, the one named last changes fastest.
Arguments:
- latents: bfloat16 [8, 2, 4, 16, 384], P(('grp', 'strm'), None, 'band'), parts along dimension 0, may hold values from -6 to 6
- cache_first: bfloat16 [8, 2, 4, 16, 384], P(('grp', 'strm'), None, 'band'), parts along dimension 0, may hold values from -6 to 6
- cache_second: bfloat16 [8, 2, 8, 32, 192], P(('grp', 'strm'), None, 'band'), parts along dimension 0, may hold values from -6 to 6
- gain_first: float32 [384], replicated, may hold values from 0.25 to 1.75
- gain_second: float32 [192], replicated, may hold values from 0.25 to 1.75
- w_first: bfloat16 [3, 3, 3, 384, 768], P(None, None, None, None, 'strm'), may hold values from -0.0625 to 0.0625
- w_second: bfloat16 [3, 3, 3, 192, 192], P(None, None, None, None, 'strm'), may hold values from -0.078125 to 0.078125
- cache_slot: int32 [8], P('grp'), parts along dimension 0, may hold values from 0 to 3, as said below
- block_index: int32 [8], P('grp'), parts along dimension 0, may hold values from 0 to 3, as said below
Outputs:
- decoded: bfloat16 [8, 2, 8, 32, 192], P(('grp', 'strm'), None, 'band'), parts along dimension 0
There are 2 independent parts, one for each index of `grp`. A program takes and returns all parts, laid end to end along the dimension named above; an argument that names none is the same for every part. Nothing has to cross between parts.
Inputs may be any that keep to these rules, and one draw needn't show every extreme that they name: `cache_slot`: each slot holds the caches of exactly one stream. The caches are read only where block_index > 0; exactly one stream of a group has block number 0.
All inputs are finite; a program needn't handle non-finite values.
Results may differ from a plain program's by a relative error of at most 0.0056.
Values may be sent and summed in bfloat16 or wider, within the bound.
A program may use at most 64 MiB of HBM per device.

v0:
```python
import jax
import jax.numpy as jnp
from jax import lax
from jax.experimental import pallas as pl
from jax.experimental.pallas import tpu as pltpu
from jax.sharding import PartitionSpec as P

epsilon = 1e-06
MESH = pl.DeviceIdType.MESH
F32 = jnp.float32
BF16 = jnp.bfloat16


def norm_silu(values, gain):
    mean_square = jnp.mean(values * values, axis=-1, keepdims=True)
    return jax.nn.silu(values * lax.rsqrt(mean_square + epsilon) * gain)


def dot_nk(left, right):
    return lax.dot_general(left, right, (((1,), (1,)), ((), ())), preferred_element_type=F32)


def kernel(
    slot_ref, block_ref, gain1_ref, gain2_ref, lat, c1, c2, w1, w2,
    base_ref, branch_ref,
    LT, A1, A2, KA, KO, KZ, W11, W02, W2, C, ES, ER, S, U, H, RB, Q,
    loc, s1, r1, s2, r2, sc, rc, se, re, su, ru, sw, rw, sq, rq,
):
    K = (KA, KO, KZ)
    p = lax.axis_index("strm")
    h = lax.axis_index("band")
    bands = lax.axis_size("band")
    core = lax.rem(p, 2)
    half = p // 2
    mate = p + 1 - 2 * core
    over = lax.rem(p + 2, 4)
    cross = lax.rem(mate + 2, 4)
    not_top = h > 0
    not_bottom = h < bands - 1

    def load(src, dst, i):
        copy = pltpu.make_async_copy(src, dst, loc.at[i])
        copy.start()
        return copy

    lat_copy = load(lat, LT, 0)
    c1_copy = load(c1, KO.at[p], 1)
    c2_copy = load(c2, C.at[p], 2)

    barrier = pltpu.get_barrier_semaphore()
    for other in (mate, over, cross):
        pl.semaphore_signal(barrier, inc=1, device_id={"strm": other}, device_id_type=MESH)

    def greet(band):
        for other in (p, mate):
            pl.semaphore_signal(
                barrier, inc=1, device_id={"strm": other, "band": band}, device_id_type=MESH
            )

    pl.when(not_top)(lambda: greet(h - 1))
    pl.when(not_bottom)(lambda: greet(h + 1))
    w1_mid = load(w1.at[:, 1], W11, 3)
    w2_copy = load(w2, W2.at[:, pl.ds(pl.multiple_of(48 * core, 16), 48)], 6)
    w1_top = load(w1.at[:, 0], W02.at[:, :, :, pl.ds(0, 384)], 4)
    w1_bot = load(w1.at[:, 2], W02.at[:, :, :, pl.ds(384, 384)], 5)

    @pl.when(h == 0)
    def _():
        KA[...] = jnp.zeros((4, 32, 384), BF16)
        A2[2:4, :, 0:384] = jnp.zeros((2, 64, 384), BF16)
        ER[0] = jnp.zeros((2, 2, 32, 192), BF16)
        U[0] = jnp.zeros((2, 2, 2, 16, 192), BF16)

    @pl.when(h == bands - 1)
    def _():
        KZ[...] = jnp.zeros((4, 32, 384), BF16)
        A2[2:4, :, 384:768] = jnp.zeros((2, 64, 384), BF16)
        ER[1] = jnp.zeros((2, 2, 32, 192), BF16)
        U[3] = jnp.zeros((2, 2, 2, 16, 192), BF16)

    def cells(s):
        return pl.ds(pl.multiple_of(16 * s, 16), 16)

    def acts(j, s):
        if j == 1:
            return A1.at[2:4, cells(s)]
        return A2.at[2:4, cells(s), pl.ds(192 * j, 384)]

    gain1 = gain1_ref[...].reshape(1, 384)
    gain2 = gain2_ref[...].reshape(1, 192)
    lat_copy.wait()
    first_act = norm_silu(LT[...].astype(F32), gain1).astype(BF16)
    A1[2, cells(p)] = first_act[0:16]
    A1[3, cells(p)] = first_act[16:32]
    c1_copy.wait()

    peers = 3 + 2 * not_top.astype(jnp.int32) + 2 * not_bottom.astype(jnp.int32)
    pl.semaphore_wait(barrier, peers)

    def remote(src, dst, send, recv, strm, band):
        return pltpu.make_async_remote_copy(
            src_ref=src, dst_ref=dst, send_sem=send, recv_sem=recv,
            device_id={"strm": strm, "band": band}, device_id_type=MESH,
        )

    class Row:
        def __init__(self, i, j_src, j_dst, s, strm, band):
            self.parts = (
                remote(K[j_src].at[s], K[j_dst].at[s], s2.at[i], r2.at[j_dst, s], strm, band),
                remote(acts(j_src, s), acts(j_dst, s), s1.at[i], r1.at[j_dst, s], strm, band),
            )

        def start(self):
            for part in self.parts:
                part.start()

        def wait_send(self):
            for part in self.parts:
                part.wait_send()

    def arrive(j, s):
        for part in Row(0, j, j, s, mate, h).parts:
            part.wait_recv()

    near = [Row(i, 1, 1, p, d, h) for i, d in enumerate((over, cross, mate))]
    above = [Row(3 + i, 1, 2, p, d, h - 1) for i, d in enumerate((p, mate))]
    below = [Row(5 + i, 1, 0, p, d, h + 1) for i, d in enumerate((p, mate))]
    above2 = [Row(7 + i, 1, 2, over, d, h - 1) for i, d in enumerate((p, mate))]
    below2 = [Row(9 + i, 1, 0, over, d, h + 1) for i, d in enumerate((p, mate))]

    def go(rows):
        for row in rows:
            row.start()

    go(near[:2])
    pl.when(not_top)(lambda: go(above))
    pl.when(not_bottom)(lambda: go(below))
    go(near[2:])
    c2_copy.wait()
    c_over = remote(C.at[p], C.at[p], sc.at[0], rc.at[p], over, h)
    c_mate = remote(C.at[p], C.at[p], sc.at[1], rc.at[p], mate, h)
    c_over.start()
    c_mate.start()

    arrive(1, over)
    pl.when(not_top)(lambda: go(above2))
    pl.when(not_bottom)(lambda: go(below2))
    def carrive(s):
        remote(C.at[s], C.at[s], sc.at[0], rc.at[s], mate, h).wait_recv()

    carrive(over)
    c_fwd = remote(C.at[over], C.at[over], sc.at[2], rc.at[over], mate, h)
    c_fwd.start()

    arrive(1, mate)
    arrive(1, cross)

    def fill(j):
        for s in range(4):
            piece = K[j][slot_ref[s]].astype(F32)
            piece = jnp.where(block_ref[s] > 0, piece, jnp.zeros_like(piece)).astype(BF16)
            for f in range(2):
                block = piece[16 * f : 16 * f + 16]
                if j == 1:
                    A1[f, 16 * s : 16 * s + 16] = block
                else:
                    A2[f, 16 * s : 16 * s + 16, 192 * j : 192 * j + 384] = block

    fill(1)
    w1_mid.wait()
    total = [None] * 3

    def taps(stack, weight, depth):
        for i in range(3):
            rows = stack[i : i + 2].reshape(128, depth)
            for l in range(3):
                term = dot_nk(rows, weight[i, l])
                total[l] = term if total[l] is None else total[l] + term

    taps(A1, W11, 384)
    w2_copy.wait()

    def w2_rows(c):
        return W2.at[:, pl.ds(pl.multiple_of(48 * c, 16), 48)]

    w_mate = remote(w2_rows(core), w2_rows(core), sw, rw, mate, h)
    w_mate.start()

    carrive(mate)
    carrive(cross)
    rows32 = lax.broadcasted_iota(jnp.int32, (32, 32), 0)
    cols32 = lax.broadcasted_iota(jnp.int32, (32, 32), 1)
    split = jnp.where(cols32 == 2 * lax.rem(rows32, 16) + rows32 // 16, 1.0, 0.0).astype(BF16)
    weave = jnp.where(rows32 == 2 * lax.rem(cols32, 16) + cols32 // 16, 1.0, 0.0).astype(BF16)

    def place(block, frame, row, sp):
        moved = jnp.dot(split, block, preferred_element_type=F32).astype(BF16)
        H[frame, row, sp * 32 : sp * 32 + 32] = moved
        return moved

    for sp in range(2):
        s = core + 2 * sp
        chosen = C[slot_ref[s]]
        chosen = jnp.where(block_ref[s] > 0, chosen.astype(F32), 0.0).astype(BF16)
        for f in range(2):
            for row in range(2):
                ES[row, sp, f] = place(chosen[f, row], f, row + 1, sp)
    e_up = remote(ES.at[0], ER.at[1], se.at[0], re.at[1], p, h - 1)
    e_down = remote(ES.at[1], ER.at[0], se.at[1], re.at[0], p, h + 1)
    pl.when(not_top)(e_up.start)
    pl.when(not_bottom)(e_down.start)

    @pl.when(not_top)
    def _():
        for s in (p, mate, over, cross):
            arrive(0, s)

    @pl.when(not_bottom)
    def _():
        for s in (p, mate, over, cross):
            arrive(2, s)

    fill(0)
    fill(2)
    w1_top.wait()
    w1_bot.wait()
    taps(A2, W02, 768)
    column = lax.rem(lax.broadcasted_iota(jnp.int32, (128, 192), 0), 16)
    up = (
        total[1]
        + jnp.where(column == 0, 0.0, pltpu.roll(total[0], 1, 0))
        + jnp.where(column == 15, 0.0, pltpu.roll(total[2], 127, 0))
    ).astype(BF16)
    for k in range(2):
        for sp in range(2):
            for t in range(2):
                start = (t * 4 + k + 2 * sp) * 16
                S[k, sp, t] = up[start : start + 16]

    def ucopy(i, d, row, band):
        return remote(
            S.at[lax.rem(d, 2)], U.at[row, :, :, core], su.at[i], ru.at[row, half, core], d, band
        )

    u_own = [ucopy(i, d, 1 + half, h) for i, d in enumerate((over, cross, mate))]
    u_up = [ucopy(3 + i, d, 3, h - 1) for i, d in enumerate((cross, over, p, mate))]
    u_down = [ucopy(3 + i, d, 0, h + 1) for i, d in enumerate((cross, over, p, mate))]
    sends_up = jnp.logical_and(half == 0, not_top)
    sends_down = jnp.logical_and(half == 1, not_bottom)
    u_own[0].start()
    u_own[1].start()

    @pl.when(sends_up)
    def _():
        for copy in u_up:
            copy.start()

    @pl.when(sends_down)
    def _():
        for copy in u_down:
            copy.start()

    u_own[2].start()
    U[1 + half, :, :, core] = S[core]

    def wait_edge(n):
        remote(ES.at[0], ER.at[n], se.at[0], re.at[n], mate, h).wait_recv()

    pl.when(not_top)(lambda: wait_edge(0))
    pl.when(not_bottom)(lambda: wait_edge(1))
    for sp in range(2):
        for f in range(2):
            H[f, 0, sp * 32 : sp * 32 + 32] = ER[0, sp, f]
            H[f, 3, sp * 32 : sp * 32 + 32] = ER[1, sp, f]
    remote(w2_rows(1 - core), w2_rows(1 - core), sw, rw, mate, h).wait_recv()
    partial = [None]

    def tap(i, j):
        at = i * 9 + j * 3
        term = dot_nk(
            H[i : i + 2, j : j + 2].reshape(256, 192), W2[at : at + 3].reshape(288, 192)
        )
        partial[0] = term if partial[0] is None else partial[0] + term

    for j in range(3):
        tap(0, j)

    def uarrive(row, b, a):
        remote(S.at[0], U.at[row, :, :, b], su.at[0], ru.at[row, a, b], mate, h).wait_recv()

    for b in range(2):
        for a in range(2):

            @pl.when(p != 2 * a + b)
            def _():
                uarrive(1 + a, b, a)

    def advance(row):
        x = U[row].reshape(128, 192).astype(F32)
        act = norm_silu(x, gain2).astype(BF16)
        for sp in range(2):
            for t in range(2):
                start = (sp * 2 + t) * 32
                H[2 + t, row, sp * 32 : sp * 32 + 32] = act[start : start + 32]

    advance(1)
    advance(2)
    tap(1, 1)
    tap(2, 1)

    @pl.when(not_top)
    def _():
        uarrive(0, 0, 1)
        uarrive(0, 1, 1)

    @pl.when(not_bottom)
    def _():
        uarrive(3, 0, 0)
        uarrive(3, 1, 0)

    advance(0)
    advance(3)
    for j in (0, 2):
        for i in (1, 2):
            tap(i, j)
    full = partial[0]
    y0, y1, y2 = full[:, 0:96], full[:, 96:192], full[:, 192:288]
    rows = lax.broadcasted_iota(jnp.int32, (256, 96), 0)
    even = lax.rem(rows // 16, 2) == 0
    place_w = lax.rem(rows, 16)
    before = jnp.where(
        even, jnp.where(place_w == 0, 0.0, pltpu.roll(y0, 241, 0)), pltpu.roll(y0, 16, 0)
    )
    after = jnp.where(
        even, pltpu.roll(y2, 240, 0), jnp.where(place_w == 15, 0.0, pltpu.roll(y2, 15, 0))
    )
    result = (y1 + before + after).astype(BF16)
    for ta in range(4):
        for sp in range(2):
            start = ta * 64 + sp * 32
            RB[sp, ta] = result[start : start + 32]
    q = remote(RB.at[1 - half], Q, sq, rq, over, h)
    q.start()
    for t in range(2):
        for a in range(2):
            block = U[1 + a, half, t].reshape(32, 192)
            base_ref[t, a] = jnp.dot(weave, block, preferred_element_type=F32).astype(BF16)
    mine = RB[half].astype(F32)
    q.wait_recv()
    theirs = Q[...].astype(F32)
    low = jnp.where(half == 0, mine, theirs)
    high = jnp.where(half == 0, theirs, mine)
    branch = jnp.concatenate([low, high], axis=-1).astype(BF16)
    for t in range(2):
        for a in range(2):
            woven = jnp.dot(weave, branch[t * 2 + a], preferred_element_type=F32)
            branch_ref[t, a] = woven.astype(BF16)

    q.wait_send()
    for copy in (*near, c_over, c_mate, c_fwd, w_mate, *u_own):
        copy.wait_send()

    def left(rows):
        for row in rows:
            row.wait_send()

    pl.when(not_top)(lambda: left(above + above2 + [e_up]))
    pl.when(not_bottom)(lambda: left(below + below2 + [e_down]))

    @pl.when(sends_up)
    def _():
        for copy in u_up:
            copy.wait_send()

    @pl.when(sends_down)
    def _():
        for copy in u_down:
            copy.wait_send()


def body(
    latents, cache_first, cache_second, gain_first, gain_second, w_first, w_second,
    cache_slot, block_index,
):
    any_spec = pl.BlockSpec(memory_space=pl.ANY)
    vmem = pl.BlockSpec(memory_space=pltpu.VMEM)
    smem = pl.BlockSpec(memory_space=pltpu.SMEM)
    dma = pltpu.SemaphoreType.DMA
    base, branch = pl.pallas_call(
        kernel,
        out_shape=[jax.ShapeDtypeStruct((2, 2, 32, 192), BF16)] * 2,
        in_specs=[smem, smem, vmem, vmem] + [any_spec] * 5,
        out_specs=[vmem, vmem],
        scratch_shapes=[
            pltpu.VMEM((32, 384), BF16),
            pltpu.VMEM((4, 64, 384), BF16),
            pltpu.VMEM((4, 64, 768), BF16),
            pltpu.VMEM((4, 32, 384), BF16),
            pltpu.VMEM((4, 32, 384), BF16),
            pltpu.VMEM((4, 32, 384), BF16),
            pltpu.VMEM((3, 3, 192, 384), BF16),
            pltpu.VMEM((3, 3, 192, 768), BF16),
            pltpu.VMEM((27, 96, 192), BF16),
            pltpu.VMEM((4, 2, 2, 32, 192), BF16),
            pltpu.VMEM((2, 2, 2, 32, 192), BF16),
            pltpu.VMEM((2, 2, 2, 32, 192), BF16),
            pltpu.VMEM((2, 2, 2, 16, 192), BF16),
            pltpu.VMEM((4, 2, 2, 2, 16, 192), BF16),
            pltpu.VMEM((4, 4, 64, 192), BF16),
            pltpu.VMEM((2, 4, 32, 96), BF16),
            pltpu.VMEM((4, 32, 96), BF16),
            dma((7,)),
            dma((11,)),
            dma((3, 4)),
            dma((11,)),
            dma((3, 4)),
            dma((3,)),
            dma((4,)),
            dma((2,)),
            dma((2,)),
            dma((7,)),
            dma((4, 2, 2)),
            dma,
            dma,
            dma,
            dma,
        ],
        compiler_params=pltpu.CompilerParams(
            collective_id=0, has_side_effects=True, vmem_limit_bytes=60 * 1024 * 1024
        ),
    )(
        cache_slot,
        block_index,
        gain_first,
        gain_second,
        latents.reshape(32, 384),
        cache_first.reshape(32, 384),
        cache_second.reshape(2, 2, 32, 192),
        w_first.transpose(0, 1, 2, 4, 3),
        w_second.transpose(0, 1, 2, 4, 3).reshape(27, 48, 192),
    )
    decoded = (base.astype(F32) + branch.astype(F32)).astype(BF16)
    return decoded.reshape(1, 2, 2, 32, 192)


def solution(mesh):
    in_specs = (
        P(("grp", "strm"), None, "band", None, None),
        P(("grp", "strm"), None, "band", None, None),
        P(("grp", "strm"), None, "band", None, None),
        P(),
        P(),
        P(None, None, None, None, "strm"),
        P(None, None, None, None, "strm"),
        P("grp"),
        P("grp"),
    )
    out_specs = P(("grp", "strm"), None, "band", None, None)
    return jax.shard_map(body, mesh=mesh, in_specs=in_specs, out_specs=out_specs, check_vma=False)
```

profile of v0, /device:TPU:0, one launch (start us, length us, event | category | flops | bytes accessed | tf_op | source)
XLA Modules:
  0.0 25.0 jit_solution(11420984839324718315)
XLA Ops:
  0.0 23.5 %shard_map.91 = (bf16[2,2,32,192]{3,2,1,0:T(8,128)(2,1)}, bf16[2,2,32,192]{3,2,1,0:T(8,128)(2,1)}) custom-call(s32[4]{0:T(128)} %slot_ref.1, s32[4]{0:T(128)} %block_ref.1, f32[384]{0:T(512)} %gain1_ref.1, f32[192]{0:T(256)} %gain2_ref.1, bf16[32,384]{1,0:T(8,128)(2,1)} %bitcast.12, bf16[32,384]{1,0:T(8,128)(2,1)} %bitcast.13, ...), custom_call_target="tpu_custom_call" | custom-call | tf_op jit(solution)/shard_map/pallas_call | solution.py:389
  23.5 1.5 %fusion = bf16[1,2,2,32,192]{4,3,2,1,0:T(8,128)(2,1)} fusion(bf16[2,2,32,192]{3,2,1,0:T(8,128)(2,1)} %get-tuple-element.8, bf16[2,2,32,192]{3,2,1,0:T(8,128)(2,1)} %get-tuple-element.7), kind=kLoop, calls=%fused_computation.1 | loop fusion | flops 98304 | bytes 147456 | tf_op jit(solution)/shard_map/reshape | solution.py:443
where the time goes:
time: 25.2 us; the launch traced here: 25 us
  Pallas kernels  23.5 us (93%)
  other arithmetic  1.52 us (6%)
    pallas_call x1, Pallas kernels, body(): pl.pallas_call(kernel, out_shape=[jax.ShapeDtypeStruct((2, 2, 32, 192), B...  23.5 us
    reshape x1, other arithmetic, body(): return decoded.reshape(1, 2, 2, 32, 192)  1.52 us

commit v1 on v0

--- a/solution.py
+++ b/solution.py
@@ -21,10 +21,11 @@
 
 
 def kernel(
-    slot_ref, block_ref, gain1_ref, gain2_ref, lat, c1, c2, w1, w2,
-    base_ref, branch_ref,
+    slot_hbm, block_hbm, gain1_hbm, gain2_hbm, lat, c1, c2, w1, w2,
+    out_ref, base_ref,
     LT, A1, A2, KA, KO, KZ, W11, W02, W2, C, ES, ER, S, U, H, RB, Q,
     loc, s1, r1, s2, r2, sc, rc, se, re, su, ru, sw, rw, sq, rq,
+    slot_ref, block_ref, gain1_ref, gain2_ref, gsem,
 ):
     K = (KA, KO, KZ)
     p = lax.axis_index("strm")
@@ -44,6 +45,19 @@
         return copy
 
     lat_copy = load(lat, LT, 0)
+    smalls = [
+        pltpu.make_async_copy(src, dst, gsem.at[i])
+        for i, (src, dst) in enumerate(
+            (
+                (gain1_hbm, gain1_ref),
+                (gain2_hbm, gain2_ref),
+                (slot_hbm, slot_ref),
+                (block_hbm, block_ref),
+            )
+        )
+    ]
+    for copy in smalls:
+        copy.start()
     c1_copy = load(c1, KO.at[p], 1)
     c2_copy = load(c2, C.at[p], 2)
 
@@ -86,6 +100,8 @@
             return A1.at[2:4, cells(s)]
         return A2.at[2:4, cells(s), pl.ds(192 * j, 384)]
 
+    for copy in smalls:
+        copy.wait()
     gain1 = gain1_ref[...].reshape(1, 384)
     gain2 = gain2_ref[...].reshape(1, 192)
     lat_copy.wait()
@@ -354,7 +370,7 @@
     for t in range(2):
         for a in range(2):
             woven = jnp.dot(weave, branch[t * 2 + a], preferred_element_type=F32)
-            branch_ref[t, a] = woven.astype(BF16)
+            out_ref[t, a] = (base_ref[t, a].astype(F32) + woven.astype(BF16).astype(F32)).astype(BF16)
 
     q.wait_send()
     for copy in (*near, c_over, c_mate, c_fwd, w_mate, *u_own):
@@ -376,22 +392,27 @@
     def _():
         for copy in u_down:
             copy.wait_send()
+
+
+def hbm(x):
+    return pltpu.with_memory_space_constraint(x, pltpu.HBM)
 
 
 def body(
     latents, cache_first, cache_second, gain_first, gain_second, w_first, w_second,
     cache_slot, block_index,
 ):
-    any_spec = pl.BlockSpec(memory_space=pl.ANY)
+    any_spec = pl.BlockSpec(memory_space=pltpu.HBM)
     vmem = pl.BlockSpec(memory_space=pltpu.VMEM)
     smem = pl.BlockSpec(memory_space=pltpu.SMEM)
     dma = pltpu.SemaphoreType.DMA
-    base, branch = pl.pallas_call(
+    decoded = pl.pallas_call(
         kernel,
-        out_shape=[jax.ShapeDtypeStruct((2, 2, 32, 192), BF16)] * 2,
-        in_specs=[smem, smem, vmem, vmem] + [any_spec] * 5,
-        out_specs=[vmem, vmem],
+        out_shape=jax.ShapeDtypeStruct((2, 2, 32, 192), BF16),
+        in_specs=[any_spec] * 9,
+        out_specs=vmem,
         scratch_shapes=[
+            pltpu.VMEM((2, 2, 32, 192), BF16),
             pltpu.VMEM((32, 384), BF16),
             pltpu.VMEM((4, 64, 384), BF16),
             pltpu.VMEM((4, 64, 768), BF16),
@@ -424,22 +445,26 @@
             dma,
             dma,
             dma,
+            pltpu.SMEM((4,), jnp.int32),
+            pltpu.SMEM((4,), jnp.int32),
+            pltpu.VMEM((384,), F32),
+            pltpu.VMEM((192,), F32),
+            dma((4,)),
         ],
         compiler_params=pltpu.CompilerParams(
-            collective_id=0, has_side_effects=True, vmem_limit_bytes=60 * 1024 * 1024
+            collective_id=0, has_side_effects=True, vmem_limit_bytes=40 * 1024 * 1024
         ),
     )(
-        cache_slot,
-        block_index,
-        gain_first,
-        gain_second,
-        latents.reshape(32, 384),
-        cache_first.reshape(32, 384),
-        cache_second.reshape(2, 2, 32, 192),
-        w_first.transpose(0, 1, 2, 4, 3),
-        w_second.transpose(0, 1, 2, 4, 3).reshape(27, 48, 192),
+        hbm(cache_slot),
+        hbm(block_index),
+        hbm(gain_first),
+        hbm(gain_second),
+        hbm(latents.reshape(32, 384)),
+        hbm(cache_first.reshape(32, 384)),
+        hbm(cache_second.reshape(2, 2, 32, 192)),
+        hbm(w_first.transpose(0, 1, 2, 4, 3)),
+        hbm(w_second.transpose(0, 1, 2, 4, 3).reshape(27, 48, 192)),
     )
-    decoded = (base.astype(F32) + branch.astype(F32)).astype(BF16)
     return decoded.reshape(1, 2, 2, 32, 192)
 
 

time: 25.2 us -> 22.9 us (0.909)
  other arithmetic: 1.52 us -> 0 us
  Pallas kernels: 23.5 us -> 22.1 us
  local copies, waits for them, and re-layouts: 0 us -> 0.63 us
    reshape x1 -> x0, other arithmetic: 1.52 us -> none  [body(): return decoded.reshape(1, 2, 2, 32, 192)]
    pallas_call x1, Pallas kernels: 23.5 us -> 22.1 us  [body(): pl.pallas_call(kernel, out_shape=jax.ShapeDtypeStruct((2, 2, 32, 192), BF...]
    unnamed x0 -> x1, local copies, waits for them, and re-layouts: none -> 0.63 us
where the time goes in v1:
time: 22.9 us; the launch traced here: 22.7 us
  Pallas kernels  22.1 us (97%)
  local copies, waits for them, and re-layouts  0.63 us (3%)
    pallas_call x1, Pallas kernels, body(): pl.pallas_call(kernel, out_shape=jax.ShapeDtypeStruct((2, 2, 32, 192), BF...  22.1 us
    unnamed x1, local copies, waits for them, and re-layouts  0.63 us

profile of v1, /device:TPU:0, one launch (start us, length us, event | category | flops | bytes accessed | tf_op | source)
XLA Modules:
  0.0 22.7 jit_solution(4600979410889841102)
XLA Ops:
  0.0 22.1 %shard_map.91 = bf16[2,2,32,192]{3,2,1,0:T(8,128)(2,1)S(1)} custom-call(s32[4]{0:T(128)} %slot_hbm.1, s32[4]{0:T(128)} %block_hbm.1, f32[384]{0:T(512)} %gain1_hbm.1, f32[192]{0:T(256)} %gain2_hbm.1, bf16[32,384]{1,0:T(8,128)(2,1)} %bitcast.12, bf16[32,384]{1,0:T(8,128)(2,1)} %bitcast.13, bf16[2,2,32,192]{3,2,1,0:T(8,128)(2,1)} %bitcast.11, ...), custom_call_target="tpu_custom_call" | custom-call | tf_op jit(solution)/shard_map/pallas_call | solution.py:409
  22.1 0.6 %copy.11 = bf16[1,2,2,32,192]{4,3,2,1,0:T(8,128)(2,1)} copy(bf16[1,2,2,32,192]{4,3,2,1,0:T(8,128)(2,1)S(1)} %bitcast.8) | data formatting | bytes 98304

commit v2 on v1

--- a/solution.py
+++ b/solution.py
@@ -23,7 +23,7 @@
 def kernel(
     slot_hbm, block_hbm, gain1_hbm, gain2_hbm, lat, c1, c2, w1, w2,
     out_ref, base_ref,
-    LT, A1, A2, KA, KO, KZ, W11, W02, W2, C, ES, ER, S, U, H, RB, Q,
+    LT, A1, A2, KA, KO, KZ, W11, W02, W2, C, EB, XR, S, U, H, RB, Q,
     loc, s1, r1, s2, r2, sc, rc, se, re, su, ru, sw, rw, sq, rq,
     slot_ref, block_ref, gain1_ref, gain2_ref, gsem,
 ):
@@ -78,19 +78,19 @@
     w1_top = load(w1.at[:, 0], W02.at[:, :, :, pl.ds(0, 384)], 4)
     w1_bot = load(w1.at[:, 2], W02.at[:, :, :, pl.ds(384, 384)], 5)
 
+    W2[:, 96:128] = jnp.zeros((27, 32, 192), BF16)
+
     @pl.when(h == 0)
     def _():
         KA[...] = jnp.zeros((4, 32, 384), BF16)
         A2[2:4, :, 0:384] = jnp.zeros((2, 64, 384), BF16)
-        ER[0] = jnp.zeros((2, 2, 32, 192), BF16)
-        U[0] = jnp.zeros((2, 2, 2, 16, 192), BF16)
+        XR[0] = jnp.zeros((2, 2, 32, 128), BF16)
 
     @pl.when(h == bands - 1)
     def _():
         KZ[...] = jnp.zeros((4, 32, 384), BF16)
         A2[2:4, :, 384:768] = jnp.zeros((2, 64, 384), BF16)
-        ER[1] = jnp.zeros((2, 2, 32, 192), BF16)
-        U[3] = jnp.zeros((2, 2, 2, 16, 192), BF16)
+        XR[1] = jnp.zeros((2, 2, 32, 128), BF16)
 
     def cells(s):
         return pl.ds(pl.multiple_of(16 * s, 16), 16)
@@ -212,7 +212,6 @@
     def place(block, frame, row, sp):
         moved = jnp.dot(split, block, preferred_element_type=F32).astype(BF16)
         H[frame, row, sp * 32 : sp * 32 + 32] = moved
-        return moved
 
     for sp in range(2):
         s = core + 2 * sp
@@ -220,11 +219,7 @@
         chosen = jnp.where(block_ref[s] > 0, chosen.astype(F32), 0.0).astype(BF16)
         for f in range(2):
             for row in range(2):
-                ES[row, sp, f] = place(chosen[f, row], f, row + 1, sp)
-    e_up = remote(ES.at[0], ER.at[1], se.at[0], re.at[1], p, h - 1)
-    e_down = remote(ES.at[1], ER.at[0], se.at[1], re.at[0], p, h + 1)
-    pl.when(not_top)(e_up.start)
-    pl.when(not_bottom)(e_down.start)
+                place(chosen[f, row], f, row, sp)
 
     @pl.when(not_top)
     def _():
@@ -248,129 +243,137 @@
         + jnp.where(column == 15, 0.0, pltpu.roll(total[2], 127, 0))
     ).astype(BF16)
     for k in range(2):
-        for sp in range(2):
-            for t in range(2):
-                start = (t * 4 + k + 2 * sp) * 16
-                S[k, sp, t] = up[start : start + 16]
-
-    def ucopy(i, d, row, band):
+        for t in range(2):
+            lo, hi = (up[(t * 4 + k + n) * 16 : (t * 4 + k + n) * 16 + 16] for n in (0, 2))
+            S[k, t, :, 0:128] = lo[:, 0:128]
+            S[k, t, :, 128:256] = hi[:, 0:128]
+            S[k, t, :, 256:384] = jnp.concatenate([lo[:, 128:192], hi[:, 128:192]], axis=-1)
+
+    def ucopy(i, d):
         return remote(
-            S.at[lax.rem(d, 2)], U.at[row, :, :, core], su.at[i], ru.at[row, half, core], d, band
-        )
-
-    u_own = [ucopy(i, d, 1 + half, h) for i, d in enumerate((over, cross, mate))]
-    u_up = [ucopy(3 + i, d, 3, h - 1) for i, d in enumerate((cross, over, p, mate))]
-    u_down = [ucopy(3 + i, d, 0, h + 1) for i, d in enumerate((cross, over, p, mate))]
-    sends_up = jnp.logical_and(half == 0, not_top)
-    sends_down = jnp.logical_and(half == 1, not_bottom)
-    u_own[0].start()
-    u_own[1].start()
-
-    @pl.when(sends_up)
-    def _():
-        for copy in u_up:
-            copy.start()
-
-    @pl.when(sends_down)
-    def _():
-        for copy in u_down:
-            copy.start()
-
-    u_own[2].start()
-    U[1 + half, :, :, core] = S[core]
-
-    def wait_edge(n):
-        remote(ES.at[0], ER.at[n], se.at[0], re.at[n], mate, h).wait_recv()
-
-    pl.when(not_top)(lambda: wait_edge(0))
-    pl.when(not_bottom)(lambda: wait_edge(1))
-    for sp in range(2):
-        for f in range(2):
-            H[f, 0, sp * 32 : sp * 32 + 32] = ER[0, sp, f]
-            H[f, 3, sp * 32 : sp * 32 + 32] = ER[1, sp, f]
+            S.at[lax.rem(d, 2)], U.at[half, :, core], su.at[i], ru.at[half, core], d, h
+        )
+
+    u_own = [ucopy(i, d) for i, d in enumerate((over, cross, mate))]
+    for copy in u_own:
+        copy.start()
+    U[half, :, core] = S[core]
     remote(w2_rows(1 - core), w2_rows(1 - core), sw, rw, mate, h).wait_recv()
-    partial = [None]
-
-    def tap(i, j):
+    def taps2(i, j, frames):
+        n = len(frames)
         at = i * 9 + j * 3
         term = dot_nk(
-            H[i : i + 2, j : j + 2].reshape(256, 192), W2[at : at + 3].reshape(288, 192)
-        )
-        partial[0] = term if partial[0] is None else partial[0] + term
-
+            H[frames[0] : frames[0] + n].reshape(n * 128, 192), W2[at : at + 3].reshape(384, 192)
+        )
+        return term
+
+    first = [[None] * 3 for _ in range(2)]
     for j in range(3):
-        tap(0, j)
-
-    def uarrive(row, b, a):
-        remote(S.at[0], U.at[row, :, :, b], su.at[0], ru.at[row, a, b], mate, h).wait_recv()
+        both = taps2(0, j, (0, 1))
+        first[0][j] = both[0:128] + taps2(1, j, (1,))
+        first[1][j] = both[128:256]
+
+    def uarrive(b, a):
+        remote(S.at[0], U.at[a, :, b], su.at[0], ru.at[a, b], mate, h).wait_recv()
 
     for b in range(2):
         for a in range(2):
 
             @pl.when(p != 2 * a + b)
             def _():
-                uarrive(1 + a, b, a)
+                uarrive(b, a)
 
     def advance(row):
-        x = U[row].reshape(128, 192).astype(F32)
-        act = norm_silu(x, gain2).astype(BF16)
+        x = U[row].reshape(64, 384).astype(F32)
+        parts = (
+            jnp.concatenate([x[:, 0:128], x[:, 256:320]], axis=-1),
+            jnp.concatenate([x[:, 128:256], x[:, 320:384]], axis=-1),
+        )
+        own = jnp.where(half == 0, parts[0], parts[1])
+        for t in range(2):
+            base_ref[t, row] = own[32 * t : 32 * t + 32]
         for sp in range(2):
+            act = norm_silu(parts[sp], gain2).astype(BF16)
             for t in range(2):
-                start = (sp * 2 + t) * 32
-                H[2 + t, row, sp * 32 : sp * 32 + 32] = act[start : start + 32]
-
+                H[2 + t, row, sp * 32 : sp * 32 + 32] = act[32 * t : 32 * t + 32]
+
+    advance(0)
     advance(1)
-    advance(2)
-    tap(1, 1)
-    tap(2, 1)
-
-    @pl.when(not_top)
-    def _():
-        uarrive(0, 0, 1)
-        uarrive(0, 1, 1)
-
-    @pl.when(not_bottom)
-    def _():
-        uarrive(3, 0, 0)
-        uarrive(3, 1, 0)
-
-    advance(0)
-    advance(3)
-    for j in (0, 2):
-        for i in (1, 2):
-            tap(i, j)
-    full = partial[0]
-    y0, y1, y2 = full[:, 0:96], full[:, 96:192], full[:, 192:288]
-    rows = lax.broadcasted_iota(jnp.int32, (256, 96), 0)
-    even = lax.rem(rows // 16, 2) == 0
-    place_w = lax.rem(rows, 16)
-    before = jnp.where(
-        even, jnp.where(place_w == 0, 0.0, pltpu.roll(y0, 241, 0)), pltpu.roll(y0, 16, 0)
-    )
-    after = jnp.where(
-        even, pltpu.roll(y2, 240, 0), jnp.where(place_w == 15, 0.0, pltpu.roll(y2, 15, 0))
-    )
-    result = (y1 + before + after).astype(BF16)
-    for ta in range(4):
-        for sp in range(2):
-            start = ta * 64 + sp * 32
-            RB[sp, ta] = result[start : start + 32]
+
+    def total2(j):
+        both = taps2(2, j, (2, 3))
+        return (first[0][j] + both[0:128], first[1][j] + both[128:256] + taps2(1, j, (2,)))
+
+    def weave_columns(full):
+        count = full.shape[0]
+        y0, y1, y2 = full[:, 0:128], full[:, 128:256], full[:, 256:384]
+        rows = lax.broadcasted_iota(jnp.int32, (count, 128), 0)
+        even = lax.rem(rows // 16, 2) == 0
+        place_w = lax.rem(rows, 16)
+        before = jnp.where(
+            even,
+            jnp.where(place_w == 0, 0.0, pltpu.roll(y0, count - 15, 0)),
+            pltpu.roll(y0, 16, 0),
+        )
+        after = jnp.where(
+            even,
+            pltpu.roll(y2, count - 16, 0),
+            jnp.where(place_w == 15, 0.0, pltpu.roll(y2, 15, 0)),
+        )
+        return y1 + before + after
+
+    def edge(n, totals):
+        for t in range(2):
+            result = weave_columns(totals[t][64 * n : 64 * n + 64]).astype(BF16)
+            for sp in range(2):
+                EB[n, sp, t] = result[32 * sp : 32 * sp + 32]
+
+    def ecopies(n, band):
+        return [
+            remote(EB.at[n, sp], XR.at[1 - n, half], se.at[n, i], re.at[1 - n, half], d, band)
+            for i, (sp, d) in enumerate(((1 - half, over), (half, p)))
+        ]
+
+    e_up = ecopies(0, h - 1)
+    e_down = ecopies(1, h + 1)
+
+    def launch(copies):
+        for copy in copies:
+            copy.start()
+
+    low_taps = total2(2)
+    edge(0, low_taps)
+    pl.when(not_top)(lambda: launch(e_up))
+    high_taps = total2(0)
+    edge(1, high_taps)
+    pl.when(not_bottom)(lambda: launch(e_down))
+    mid_taps = total2(1)
+    mine = [[None] * 2 for _ in range(2)]
+    for t in range(2):
+        for a in range(2):
+            other = low_taps[t][64:128] if a == 0 else high_taps[t][0:64]
+            result = weave_columns(mid_taps[t][64 * a : 64 * a + 64] + other)
+            for sp in range(2):
+                RB[sp, t * 2 + a] = result[32 * sp : 32 * sp + 32].astype(BF16)
+            mine[t][a] = jnp.where(half == 0, result[0:32], result[32:64])
     q = remote(RB.at[1 - half], Q, sq, rq, over, h)
     q.start()
+
+    def earrive(n):
+        for g in range(2):
+            remote(EB.at[0, 0], XR.at[n, g], se.at[0, 0], re.at[n, g], over, h).wait_recv()
+
+    pl.when(not_top)(lambda: earrive(0))
+    pl.when(not_bottom)(lambda: earrive(1))
+    q.wait_recv()
     for t in range(2):
         for a in range(2):
-            block = U[1 + a, half, t].reshape(32, 192)
-            base_ref[t, a] = jnp.dot(weave, block, preferred_element_type=F32).astype(BF16)
-    mine = RB[half].astype(F32)
-    q.wait_recv()
-    theirs = Q[...].astype(F32)
-    low = jnp.where(half == 0, mine, theirs)
-    high = jnp.where(half == 0, theirs, mine)
-    branch = jnp.concatenate([low, high], axis=-1).astype(BF16)
-    for t in range(2):
-        for a in range(2):
-            woven = jnp.dot(weave, branch[t * 2 + a], preferred_element_type=F32)
-            out_ref[t, a] = (base_ref[t, a].astype(F32) + woven.astype(BF16).astype(F32)).astype(BF16)
+            theirs = Q[t * 2 + a].astype(F32)
+            low = jnp.where(half == 0, mine[t][a], theirs) + XR[a, 0, t].astype(F32)
+            high = jnp.where(half == 0, theirs, mine[t][a]) + XR[a, 1, t].astype(F32)
+            branch = jnp.concatenate([low[:, 0:96], high[:, 0:96]], axis=-1).astype(BF16)
+            total_ta = (base_ref[t, a] + branch.astype(F32)).astype(BF16)
+            out_ref[t, a] = jnp.dot(weave, total_ta, preferred_element_type=F32).astype(BF16)
 
     q.wait_send()
     for copy in (*near, c_over, c_mate, c_fwd, w_mate, *u_own):
@@ -380,18 +383,8 @@
         for row in rows:
             row.wait_send()
 
-    pl.when(not_top)(lambda: left(above + above2 + [e_up]))
-    pl.when(not_bottom)(lambda: left(below + below2 + [e_down]))
-
-    @pl.when(sends_up)
-    def _():
-        for copy in u_up:
-            copy.wait_send()
-
-    @pl.when(sends_down)
-    def _():
-        for copy in u_down:
-            copy.wait_send()
+    pl.when(not_top)(lambda: left(above + above2 + e_up))
+    pl.when(not_bottom)(lambda: left(below + below2 + e_down))
 
 
 def hbm(x):
@@ -412,7 +405,7 @@
         in_specs=[any_spec] * 9,
         out_specs=vmem,
         scratch_shapes=[
-            pltpu.VMEM((2, 2, 32, 192), BF16),
+            pltpu.VMEM((2, 2, 32, 192), F32),
             pltpu.VMEM((32, 384), BF16),
             pltpu.VMEM((4, 64, 384), BF16),
             pltpu.VMEM((4, 64, 768), BF16),
@@ -421,15 +414,15 @@
             pltpu.VMEM((4, 32, 384), BF16),
             pltpu.VMEM((3, 3, 192, 384), BF16),
             pltpu.VMEM((3, 3, 192, 768), BF16),
-            pltpu.VMEM((27, 96, 192), BF16),
+            pltpu.VMEM((27, 128, 192), BF16),
             pltpu.VMEM((4, 2, 2, 32, 192), BF16),
-            pltpu.VMEM((2, 2, 2, 32, 192), BF16),
-            pltpu.VMEM((2, 2, 2, 32, 192), BF16),
-            pltpu.VMEM((2, 2, 2, 16, 192), BF16),
-            pltpu.VMEM((4, 2, 2, 2, 16, 192), BF16),
-            pltpu.VMEM((4, 4, 64, 192), BF16),
-            pltpu.VMEM((2, 4, 32, 96), BF16),
-            pltpu.VMEM((4, 32, 96), BF16),
+            pltpu.VMEM((2, 2, 2, 32, 128), BF16),
+            pltpu.VMEM((2, 2, 2, 32, 128), BF16),
+            pltpu.VMEM((2, 2, 16, 384), BF16),
+            pltpu.VMEM((2, 2, 2, 16, 384), BF16),
+            pltpu.VMEM((4, 2, 64, 192), BF16),
+            pltpu.VMEM((2, 4, 32, 128), BF16),
+            pltpu.VMEM((4, 32, 128), BF16),
             dma((7,)),
             dma((11,)),
             dma((3, 4)),
@@ -437,10 +430,10 @@
             dma((3, 4)),
             dma((3,)),
             dma((4,)),
-            dma((2,)),
-            dma((2,)),
-            dma((7,)),
-            dma((4, 2, 2)),
+            dma((2, 2)),
+            dma((2, 2)),
+            dma((3,)),
+            dma((2, 2)),
             dma,
             dma,
             dma,

time: 22.9 us -> 21.2 us (0.926)
  Pallas kernels: 22.1 us -> 20.4 us
    pallas_call x1, Pallas kernels: 22.1 us -> 20.4 us  [body(): pl.pallas_call(kernel, out_shape=jax.ShapeDtypeStruct((2, 2, 32, 192), BF...]
where the time goes in v2:
time: 21.2 us; the launch traced here: 21.1 us
  Pallas kernels  20.4 us (96%)
  local copies, waits for them, and re-layouts  0.63 us (3%)
    pallas_call x1, Pallas kernels, body(): pl.pallas_call(kernel, out_shape=jax.ShapeDtypeStruct((2, 2, 32, 192), BF...  20.4 us
    unnamed x1, local copies, waits for them, and re-layouts  0.63 us

profile of v2, /device:TPU:0, one launch (start us, length us, event | category | flops | bytes accessed | tf_op | source)
XLA Modules:
  0.0 21.1 jit_solution(8448832095408952799)
XLA Ops:
  0.0 20.4 %shard_map.91 = bf16[2,2,32,192]{3,2,1,0:T(8,128)(2,1)S(1)} custom-call(s32[4]{0:T(128)} %slot_hbm.1, s32[4]{0:T(128)} %block_hbm.1, f32[384]{0:T(512)} %gain1_hbm.1, f32[192]{0:T(256)} %gain2_hbm.1, bf16[32,384]{1,0:T(8,128)(2,1)} %bitcast.12, bf16[32,384]{1,0:T(8,128)(2,1)} %bitcast.13, bf16[2,2,32,192]{3,2,1,0:T(8,128)(2,1)} %bitcast.11, ...), custom_call_target="tpu_custom_call" | custom-call | tf_op jit(solution)/shard_map/pallas_call | solution.py:402
  20.4 0.6 %copy.11 = bf16[1,2,2,32,192]{4,3,2,1,0:T(8,128)(2,1)} copy(bf16[1,2,2,32,192]{4,3,2,1,0:T(8,128)(2,1)S(1)} %bitcast.8) | data formatting | bytes 98304

commit v3 on v2

--- a/solution.py
+++ b/solution.py
@@ -23,11 +23,10 @@
 def kernel(
     slot_hbm, block_hbm, gain1_hbm, gain2_hbm, lat, c1, c2, w1, w2,
     out_ref, base_ref,
-    LT, A1, A2, KA, KO, KZ, W11, W02, W2, C, EB, XR, S, U, H, RB, Q,
-    loc, s1, r1, s2, r2, sc, rc, se, re, su, ru, sw, rw, sq, rq,
+    LT, A1, KO, W1, W2, C, EA, XA, EB, XR, S, U, H, RB, Q,
+    loc, s1, r1, s2, r2, sc, rc, sa, ra, se, re, su, ru, sw, rw, sq, rq,
     slot_ref, block_ref, gain1_ref, gain2_ref, gsem,
 ):
-    K = (KA, KO, KZ)
     p = lax.axis_index("strm")
     h = lax.axis_index("band")
     bands = lax.axis_size("band")
@@ -59,46 +58,33 @@
     for copy in smalls:
         copy.start()
     c1_copy = load(c1, KO.at[p], 1)
-    c2_copy = load(c2, C.at[p], 2)
 
     barrier = pltpu.get_barrier_semaphore()
     for other in (mate, over, cross):
         pl.semaphore_signal(barrier, inc=1, device_id={"strm": other}, device_id_type=MESH)
 
     def greet(band):
-        for other in (p, mate):
-            pl.semaphore_signal(
-                barrier, inc=1, device_id={"strm": other, "band": band}, device_id_type=MESH
-            )
+        pl.semaphore_signal(barrier, inc=1, device_id={"band": band}, device_id_type=MESH)
 
     pl.when(not_top)(lambda: greet(h - 1))
     pl.when(not_bottom)(lambda: greet(h + 1))
-    w1_mid = load(w1.at[:, 1], W11, 3)
+    c2_copy = load(c2, C.at[p], 2)
+    w1_copies = {j: load(w1.at[:, j], W1.at[j], 3 + j) for j in (2, 0, 1)}
     w2_copy = load(w2, W2.at[:, pl.ds(pl.multiple_of(48 * core, 16), 48)], 6)
-    w1_top = load(w1.at[:, 0], W02.at[:, :, :, pl.ds(0, 384)], 4)
-    w1_bot = load(w1.at[:, 2], W02.at[:, :, :, pl.ds(384, 384)], 5)
-
     W2[:, 96:128] = jnp.zeros((27, 32, 192), BF16)
 
     @pl.when(h == 0)
     def _():
-        KA[...] = jnp.zeros((4, 32, 384), BF16)
-        A2[2:4, :, 0:384] = jnp.zeros((2, 64, 384), BF16)
+        XA[0] = jnp.zeros((2, 2, 16, 384), BF16)
         XR[0] = jnp.zeros((2, 2, 32, 128), BF16)
 
     @pl.when(h == bands - 1)
     def _():
-        KZ[...] = jnp.zeros((4, 32, 384), BF16)
-        A2[2:4, :, 384:768] = jnp.zeros((2, 64, 384), BF16)
+        XA[1] = jnp.zeros((2, 2, 16, 384), BF16)
         XR[1] = jnp.zeros((2, 2, 32, 128), BF16)
 
     def cells(s):
         return pl.ds(pl.multiple_of(16 * s, 16), 16)
-
-    def acts(j, s):
-        if j == 1:
-            return A1.at[2:4, cells(s)]
-        return A2.at[2:4, cells(s), pl.ds(192 * j, 384)]
 
     for copy in smalls:
         copy.wait()
@@ -110,7 +96,7 @@
     A1[3, cells(p)] = first_act[16:32]
     c1_copy.wait()
 
-    peers = 3 + 2 * not_top.astype(jnp.int32) + 2 * not_bottom.astype(jnp.int32)
+    peers = 3 + not_top.astype(jnp.int32) + not_bottom.astype(jnp.int32)
     pl.semaphore_wait(barrier, peers)
 
     def remote(src, dst, send, recv, strm, band):
@@ -119,88 +105,110 @@
             device_id={"strm": strm, "band": band}, device_id_type=MESH,
         )
 
-    class Row:
-        def __init__(self, i, j_src, j_dst, s, strm, band):
-            self.parts = (
-                remote(K[j_src].at[s], K[j_dst].at[s], s2.at[i], r2.at[j_dst, s], strm, band),
-                remote(acts(j_src, s), acts(j_dst, s), s1.at[i], r1.at[j_dst, s], strm, band),
-            )
-
-        def start(self):
-            for part in self.parts:
-                part.start()
-
-        def wait_send(self):
-            for part in self.parts:
-                part.wait_send()
-
-    def arrive(j, s):
-        for part in Row(0, j, j, s, mate, h).parts:
-            part.wait_recv()
-
-    near = [Row(i, 1, 1, p, d, h) for i, d in enumerate((over, cross, mate))]
-    above = [Row(3 + i, 1, 2, p, d, h - 1) for i, d in enumerate((p, mate))]
-    below = [Row(5 + i, 1, 0, p, d, h + 1) for i, d in enumerate((p, mate))]
-    above2 = [Row(7 + i, 1, 2, over, d, h - 1) for i, d in enumerate((p, mate))]
-    below2 = [Row(9 + i, 1, 0, over, d, h + 1) for i, d in enumerate((p, mate))]
-
-    def go(rows):
-        for row in rows:
-            row.start()
-
-    go(near[:2])
-    pl.when(not_top)(lambda: go(above))
-    pl.when(not_bottom)(lambda: go(below))
-    go(near[2:])
+    def kcopy(i, s, d):
+        return remote(KO.at[s], KO.at[s], s2.at[i], r2.at[s], d, h)
+
+    def acopy(i, s, d):
+        rows = A1.at[2:4, cells(s)]
+        return remote(rows, rows, s1.at[i], r1.at[s], d, h)
+
+    def launch(copies):
+        for copy in copies:
+            copy.start()
+
+    near = [make(i, p, d) for make in (kcopy, acopy) for i, d in enumerate((over, cross, mate))]
+    launch(near)
     c2_copy.wait()
     c_over = remote(C.at[p], C.at[p], sc.at[0], rc.at[p], over, h)
     c_mate = remote(C.at[p], C.at[p], sc.at[1], rc.at[p], mate, h)
     c_over.start()
     c_mate.start()
 
-    arrive(1, over)
-    pl.when(not_top)(lambda: go(above2))
-    pl.when(not_bottom)(lambda: go(below2))
     def carrive(s):
         remote(C.at[s], C.at[s], sc.at[0], rc.at[s], mate, h).wait_recv()
 
+    for s in (mate, over, cross):
+        kcopy(0, s, mate).wait_recv()
+    for s in range(4):
+        piece = KO[slot_ref[s]].astype(F32)
+        piece = jnp.where(block_ref[s] > 0, piece, jnp.zeros_like(piece)).astype(BF16)
+        for f in range(2):
+            A1[f, 16 * s : 16 * s + 16] = piece[16 * f : 16 * f + 16]
+
+    total = [[None] * 3 for _ in range(3)]
+
+    def taps(j, i):
+        rows = A1[i : i + 2].reshape(128, 384)
+        for l in range(3):
+            term = dot_nk(rows, W1[j, i, l])
+            total[j][l] = term if total[j][l] is None else total[j][l] + term
+
+    for j in (2, 0, 1):
+        w1_copies[j].wait()
+        taps(j, 0)
+
+    for s in (mate, over, cross):
+        acopy(0, s, mate).wait_recv()
+    column = lax.rem(lax.broadcasted_iota(jnp.int32, (128, 192), 0), 16)
+
+    def packed(j):
+        taps(j, 1)
+        taps(j, 2)
+        full = (
+            total[j][1]
+            + jnp.where(column == 0, 0.0, pltpu.roll(total[j][0], 1, 0))
+            + jnp.where(column == 15, 0.0, pltpu.roll(total[j][2], 127, 0))
+        )
+        rows = {}
+        for k in range(2):
+            for t in range(2):
+                lo, hi = (
+                    full[(t * 4 + k + n) * 16 : (t * 4 + k + n) * 16 + 16] for n in (0, 2)
+                )
+                rows[k, t] = jnp.concatenate(
+                    [lo[:, 0:128], hi[:, 0:128], lo[:, 128:192], hi[:, 128:192]], axis=-1
+                )
+        return rows
+
+    def offer(n, j):
+        for (k, t), value in packed(j).items():
+            EA[n, k, t] = value.astype(BF16)
+
+    a_up = remote(EA.at[0], XA.at[1], sa.at[0], ra.at[1], p, h - 1)
+    a_down = remote(EA.at[1], XA.at[0], sa.at[1], ra.at[0], p, h + 1)
+    offer(0, 2)
+    pl.when(not_top)(a_up.start)
+    offer(1, 0)
+    pl.when(not_bottom)(a_down.start)
+    middle = packed(1)
+
+    w2_copy.wait()
+
+    def w2_rows(c):
+        return W2.at[:, pl.ds(pl.multiple_of(48 * c, 16), 48)]
+
+    w_mate = remote(w2_rows(core), w2_rows(core), sw, rw, mate, h)
+    w_mate.start()
     carrive(over)
     c_fwd = remote(C.at[over], C.at[over], sc.at[2], rc.at[over], mate, h)
     c_fwd.start()
 
-    arrive(1, mate)
-    arrive(1, cross)
-
-    def fill(j):
-        for s in range(4):
-            piece = K[j][slot_ref[s]].astype(F32)
-            piece = jnp.where(block_ref[s] > 0, piece, jnp.zeros_like(piece)).astype(BF16)
-            for f in range(2):
-                block = piece[16 * f : 16 * f + 16]
-                if j == 1:
-                    A1[f, 16 * s : 16 * s + 16] = block
-                else:
-                    A2[f, 16 * s : 16 * s + 16, 192 * j : 192 * j + 384] = block
-
-    fill(1)
-    w1_mid.wait()
-    total = [None] * 3
-
-    def taps(stack, weight, depth):
-        for i in range(3):
-            rows = stack[i : i + 2].reshape(128, depth)
-            for l in range(3):
-                term = dot_nk(rows, weight[i, l])
-                total[l] = term if total[l] is None else total[l] + term
-
-    taps(A1, W11, 384)
-    w2_copy.wait()
-
-    def w2_rows(c):
-        return W2.at[:, pl.ds(pl.multiple_of(48 * c, 16), 48)]
-
-    w_mate = remote(w2_rows(core), w2_rows(core), sw, rw, mate, h)
-    w_mate.start()
+    def await_a(n):
+        remote(EA.at[0], XA.at[n], sa.at[0], ra.at[n], mate, h).wait_recv()
+
+    pl.when(not_top)(lambda: await_a(0))
+    pl.when(not_bottom)(lambda: await_a(1))
+    for (k, t), value in middle.items():
+        S[k, t] = (value + XA[0, k, t].astype(F32) + XA[1, k, t].astype(F32)).astype(BF16)
+
+    def ucopy(i, d):
+        return remote(
+            S.at[lax.rem(d, 2)], U.at[half, :, core], su.at[i], ru.at[half, core], d, h
+        )
+
+    u_own = [ucopy(i, d) for i, d in enumerate((over, cross, mate))]
+    launch(u_own)
+    U[half, :, core] = S[core]
 
     carrive(mate)
     carrive(cross)
@@ -209,55 +217,14 @@
     split = jnp.where(cols32 == 2 * lax.rem(rows32, 16) + rows32 // 16, 1.0, 0.0).astype(BF16)
     weave = jnp.where(rows32 == 2 * lax.rem(cols32, 16) + cols32 // 16, 1.0, 0.0).astype(BF16)
 
-    def place(block, frame, row, sp):
-        moved = jnp.dot(split, block, preferred_element_type=F32).astype(BF16)
-        H[frame, row, sp * 32 : sp * 32 + 32] = moved
-
     for sp in range(2):
         s = core + 2 * sp
         chosen = C[slot_ref[s]]
         chosen = jnp.where(block_ref[s] > 0, chosen.astype(F32), 0.0).astype(BF16)
         for f in range(2):
             for row in range(2):
-                place(chosen[f, row], f, row, sp)
-
-    @pl.when(not_top)
-    def _():
-        for s in (p, mate, over, cross):
-            arrive(0, s)
-
-    @pl.when(not_bottom)
-    def _():
-        for s in (p, mate, over, cross):
-            arrive(2, s)
-
-    fill(0)
-    fill(2)
-    w1_top.wait()
-    w1_bot.wait()
-    taps(A2, W02, 768)
-    column = lax.rem(lax.broadcasted_iota(jnp.int32, (128, 192), 0), 16)
-    up = (
-        total[1]
-        + jnp.where(column == 0, 0.0, pltpu.roll(total[0], 1, 0))
-        + jnp.where(column == 15, 0.0, pltpu.roll(total[2], 127, 0))
-    ).astype(BF16)
-    for k in range(2):
-        for t in range(2):
-            lo, hi = (up[(t * 4 + k + n) * 16 : (t * 4 + k + n) * 16 + 16] for n in (0, 2))
-            S[k, t, :, 0:128] = lo[:, 0:128]
-            S[k, t, :, 128:256] = hi[:, 0:128]
-            S[k, t, :, 256:384] = jnp.concatenate([lo[:, 128:192], hi[:, 128:192]], axis=-1)
-
-    def ucopy(i, d):
-        return remote(
-            S.at[lax.rem(d, 2)], U.at[half, :, core], su.at[i], ru.at[half, core], d, h
-        )
-
-    u_own = [ucopy(i, d) for i, d in enumerate((over, cross, mate))]
-    for copy in u_own:
-        copy.start()
-    U[half, :, core] = S[core]
+                moved = jnp.dot(split, chosen[f, row], preferred_element_type=F32).astype(BF16)
+                H[f, row, sp * 32 : sp * 32 + 32] = moved
     remote(w2_rows(1 - core), w2_rows(1 - core), sw, rw, mate, h).wait_recv()
     def taps2(i, j, frames):
         n = len(frames)
@@ -336,10 +303,6 @@
 
     e_up = ecopies(0, h - 1)
     e_down = ecopies(1, h + 1)
-
-    def launch(copies):
-        for copy in copies:
-            copy.start()
 
     low_taps = total2(2)
     edge(0, low_taps)
@@ -383,8 +346,8 @@
         for row in rows:
             row.wait_send()
 
-    pl.when(not_top)(lambda: left(above + above2 + e_up))
-    pl.when(not_bottom)(lambda: left(below + below2 + e_down))
+    pl.when(not_top)(lambda: left([a_up] + e_up))
+    pl.when(not_bottom)(lambda: left([a_down] + e_down))
 
 
 def hbm(x):
@@ -408,14 +371,12 @@
             pltpu.VMEM((2, 2, 32, 192), F32),
             pltpu.VMEM((32, 384), BF16),
             pltpu.VMEM((4, 64, 384), BF16),
-            pltpu.VMEM((4, 64, 768), BF16),
             pltpu.VMEM((4, 32, 384), BF16),
-            pltpu.VMEM((4, 32, 384), BF16),
-            pltpu.VMEM((4, 32, 384), BF16),
-            pltpu.VMEM((3, 3, 192, 384), BF16),
-            pltpu.VMEM((3, 3, 192, 768), BF16),
+            pltpu.VMEM((3, 3, 3, 192, 384), BF16),
             pltpu.VMEM((27, 128, 192), BF16),
             pltpu.VMEM((4, 2, 2, 32, 192), BF16),
+            pltpu.VMEM((2, 2, 2, 16, 384), BF16),
+            pltpu.VMEM((2, 2, 2, 16, 384), BF16),
             pltpu.VMEM((2, 2, 2, 32, 128), BF16),
             pltpu.VMEM((2, 2, 2, 32, 128), BF16),
             pltpu.VMEM((2, 2, 16, 384), BF16),
@@ -424,12 +385,14 @@
             pltpu.VMEM((2, 4, 32, 128), BF16),
             pltpu.VMEM((4, 32, 128), BF16),
             dma((7,)),
-            dma((11,)),
-            dma((3, 4)),
-            dma((11,)),
-            dma((3, 4)),
             dma((3,)),
             dma((4,)),
+            dma((3,)),
+            dma((4,)),
+            dma((3,)),
+            dma((4,)),
+            dma((2,)),
+            dma((2,)),
             dma((2, 2)),
             dma((2, 2)),
             dma((3,)),

time: 21.2 us -> 20.7 us (0.976)
  Pallas kernels: 20.4 us -> 19.9 us
    pallas_call x1, Pallas kernels: 20.4 us -> 19.9 us  [body(): pl.pallas_call(kernel, out_shape=jax.ShapeDtypeStruct((2, 2, 32, 192), BF...]
where the time goes in v3:
time: 20.7 us; the launch traced here: 20.5 us
  Pallas kernels  19.9 us (96%)
  local copies, waits for them, and re-layouts  0.63 us (3%)
    pallas_call x1, Pallas kernels, body(): pl.pallas_call(kernel, out_shape=jax.ShapeDtypeStruct((2, 2, 32, 192), BF...  19.9 us
    unnamed x1, local copies, waits for them, and re-layouts  0.63 us

profile of v3, /device:TPU:0, one launch (start us, length us, event | category | flops | bytes accessed | tf_op | source)
XLA Modules:
  0.0 20.5 jit_solution(5769200518510056335)
XLA Ops:
  0.0 19.9 %shard_map.91 = bf16[2,2,32,192]{3,2,1,0:T(8,128)(2,1)S(1)} custom-call(s32[4]{0:T(128)} %slot_hbm.1, s32[4]{0:T(128)} %block_hbm.1, f32[384]{0:T(512)} %gain1_hbm.1, f32[192]{0:T(256)} %gain2_hbm.1, bf16[32,384]{1,0:T(8,128)(2,1)} %bitcast.12, bf16[32,384]{1,0:T(8,128)(2,1)} %bitcast.13, bf16[2,2,32,192]{3,2,1,0:T(8,128)(2,1)} %bitcast.11, ...), custom_call_target="tpu_custom_call" | custom-call | tf_op jit(solution)/shard_map/pallas_call | solution.py:365
  19.9 0.6 %copy.11 = bf16[1,2,2,32,192]{4,3,2,1,0:T(8,128)(2,1)} copy(bf16[1,2,2,32,192]{4,3,2,1,0:T(8,128)(2,1)S(1)} %bitcast.8) | data formatting | bytes 98304

commit v4 on v3

--- a/solution.py
+++ b/solution.py
@@ -23,7 +23,7 @@
 def kernel(
     slot_hbm, block_hbm, gain1_hbm, gain2_hbm, lat, c1, c2, w1, w2,
     out_ref, base_ref,
-    LT, A1, KO, W1, W2, C, EA, XA, EB, XR, S, U, H, RB, Q,
+    LT, A1, KO, WA, WB, T, W2, C, EA, XA, EB, XR, S, U, H, RB, Q,
     loc, s1, r1, s2, r2, sc, rc, sa, ra, se, re, su, ru, sw, rw, sq, rq,
     slot_ref, block_ref, gain1_ref, gain2_ref, gsem,
 ):
@@ -69,7 +69,11 @@
     pl.when(not_top)(lambda: greet(h - 1))
     pl.when(not_bottom)(lambda: greet(h + 1))
     c2_copy = load(c2, C.at[p], 2)
-    w1_copies = {j: load(w1.at[:, j], W1.at[j], 3 + j) for j in (2, 0, 1)}
+    w1_copies = (
+        load(w1.at[0], WA, 3),
+        load(w1.at[1], WB.at[:, :, :, pl.ds(0, 384)], 4),
+        load(w1.at[2], WB.at[:, :, :, pl.ds(384, 384)], 5),
+    )
     w2_copy = load(w2, W2.at[:, pl.ds(pl.multiple_of(48 * core, 16), 48)], 6)
     W2[:, 96:128] = jnp.zeros((27, 32, 192), BF16)
 
@@ -135,29 +139,27 @@
         for f in range(2):
             A1[f, 16 * s : 16 * s + 16] = piece[16 * f : 16 * f + 16]
 
-    total = [[None] * 3 for _ in range(3)]
-
-    def taps(j, i):
-        rows = A1[i : i + 2].reshape(128, 384)
+    w1_copies[0].wait()
+    cached = A1[0:2].reshape(128, 384)
+    for j in (2, 0, 1):
         for l in range(3):
-            term = dot_nk(rows, W1[j, i, l])
-            total[j][l] = term if total[j][l] is None else total[j][l] + term
-
-    for j in (2, 0, 1):
-        w1_copies[j].wait()
-        taps(j, 0)
+            T[j, l] = dot_nk(cached, WA[j, l])
+    w1_copies[1].wait()
+    w1_copies[2].wait()
 
     for s in (mate, over, cross):
         acopy(0, s, mate).wait_recv()
+    recent = jnp.concatenate(
+        [A1[1:3].reshape(128, 384), A1[2:4].reshape(128, 384)], axis=-1
+    )
     column = lax.rem(lax.broadcasted_iota(jnp.int32, (128, 192), 0), 16)
 
     def packed(j):
-        taps(j, 1)
-        taps(j, 2)
+        total = [T[j, l] + dot_nk(recent, WB[j, l]) for l in range(3)]
         full = (
-            total[j][1]
-            + jnp.where(column == 0, 0.0, pltpu.roll(total[j][0], 1, 0))
-            + jnp.where(column == 15, 0.0, pltpu.roll(total[j][2], 127, 0))
+            total[1]
+            + jnp.where(column == 0, 0.0, pltpu.roll(total[0], 1, 0))
+            + jnp.where(column == 15, 0.0, pltpu.roll(total[2], 127, 0))
         )
         rows = {}
         for k in range(2):
@@ -372,7 +374,9 @@
             pltpu.VMEM((32, 384), BF16),
             pltpu.VMEM((4, 64, 384), BF16),
             pltpu.VMEM((4, 32, 384), BF16),
-            pltpu.VMEM((3, 3, 3, 192, 384), BF16),
+            pltpu.VMEM((3, 3, 192, 384), BF16),
+            pltpu.VMEM((3, 3, 192, 768), BF16),
+            pltpu.VMEM((3, 3, 128, 192), F32),
             pltpu.VMEM((27, 128, 192), BF16),
             pltpu.VMEM((4, 2, 2, 32, 192), BF16),
             pltpu.VMEM((2, 2, 2, 16, 384), BF16),

time: 20.7 us -> 20.3 us (0.981)
  Pallas kernels: 19.9 us -> 19.6 us
    pallas_call x1, Pallas kernels: 19.9 us -> 19.6 us  [body(): pl.pallas_call(kernel, out_shape=jax.ShapeDtypeStruct((2, 2, 32, 192), BF...]
where the time goes in v4:
time: 20.3 us; the launch traced here: 20.2 us
  Pallas kernels  19.6 us (97%)
  local copies, waits for them, and re-layouts  0.63 us (3%)
    pallas_call x1, Pallas kernels, body(): pl.pallas_call(kernel, out_shape=jax.ShapeDtypeStruct((2, 2, 32, 192), BF...  19.6 us
    unnamed x1, local copies, waits for them, and re-layouts  0.63 us

profile of v4, /device:TPU:0, one launch (start us, length us, event | category | flops | bytes accessed | tf_op | source)
XLA Modules:
  0.0 20.2 jit_solution(8482980551121337698)
XLA Ops:
  0.0 19.6 %shard_map.91 = bf16[2,2,32,192]{3,2,1,0:T(8,128)(2,1)S(1)} custom-call(s32[4]{0:T(128)} %slot_hbm.1, s32[4]{0:T(128)} %block_hbm.1, f32[384]{0:T(512)} %gain1_hbm.1, f32[192]{0:T(256)} %gain2_hbm.1, bf16[32,384]{1,0:T(8,128)(2,1)} %bitcast.12, bf16[32,384]{1,0:T(8,128)(2,1)} %bitcast.13, bf16[2,2,32,192]{3,2,1,0:T(8,128)(2,1)} %bitcast.11, ...), custom_call_target="tpu_custom_call" | custom-call | tf_op jit(solution)/shard_map/pallas_call | solution.py:367
  19.6 0.6 %copy.11 = bf16[1,2,2,32,192]{4,3,2,1,0:T(8,128)(2,1)} copy(bf16[1,2,2,32,192]{4,3,2,1,0:T(8,128)(2,1)S(1)} %bitcast.8) | data formatting | bytes 98304
